TPU v7x, 32 devices: a whole 2x2x4 slice. The times are simulated.
32 devices in a mesh: ctx: 16 (over z, x, core), head: 2 (over y).
Axes of the slice: x: 2, y: 2, z: 4, core: 2. Of those that a mesh axis runs over, the one named last changes fastest.
Arguments:
- features: float32 [4096, 8192], P(('ctx', 'head')), may hold values from -200 to 200
- state_write: float32 [4096, 1024], P(('ctx', 'head')), may hold values from -6 to 6
- state_read: float32 [4096, 1024], P(('ctx', 'head')), may hold values from -6 to 6
- log_decay: float32 [4096, 128], P(('ctx', 'head')), may hold values from -0.6932 to 0, as said below
- conv_features: float32 [4, 8192], replicated, may hold values from -3 to 3
- conv_write: float32 [4, 1024], replicated, may hold values from -3 to 3
- conv_read: float32 [4, 1024], replicated, may hold values from -3 to 3
- norm_gain: float32 [8192], P('head'), may hold values from 0.5 to 1.5
Outputs:
- normed_head_outputs: float32 [4096, 8192], P('ctx', 'head')
Inputs may be any that keep to these rules, and one draw needn't show every extreme that they name: `log_decay`: strictly negative.
All inputs are finite; a program needn't handle non-finite values.
Results may differ from a plain program's by a relative error of at most 0.00029.
Values sent between devices are 32-bit elements; how exact they have to be, the bound alone decides.
A program may use at most 128 MiB of HBM per device.

v0:
```python
import jax
import jax.numpy as jnp
from jax import lax
from jax.sharding import PartitionSpec as P

H = 128
P_SIZE = 64
N = 128
G = 8
BLOCK = 256


highest = lax.Precision.HIGHEST
eps_norm = 1e-05


def passed_along(value, axis, steps):
    count = lax.axis_size(axis)
    leading, last = (max(0, -steps), min(count, count - steps))
    return lax.ppermute(value, axis, [(source, source + steps) for source in range(leading, last)])


def causal_conv(tokens, leading, weight):
    tap_count = weight.shape[0]
    padded = jnp.concatenate([leading, tokens], 0)
    extent = tokens.shape[0]
    summed = weight[0] * padded[0:extent]
    for displacement in range(1, tap_count):
        summed = summed + weight[displacement] * padded[displacement : displacement + extent]
    return jax.nn.silu(summed)


def block_pass(carried_state, blocked):
    inputs_act, writes_act, reads_act, decays = blocked
    cumulative = jnp.cumsum(decays, 0)
    extent = decays.shape[0]
    target = lax.broadcasted_iota(jnp.int32, (extent, extent), 0)
    source = lax.broadcasted_iota(jnp.int32, (extent, extent), 1)
    strictly_past = target >= source
    along = jnp.transpose(cumulative, (1, 2, 0))
    spacing = jnp.where(strictly_past, along[..., :, None] - along[..., None, :], 0.0)
    damping = jnp.where(strictly_past, jnp.exp(spacing), 0.0)
    scores = jnp.einsum("tgn,sgn->gts", reads_act, writes_act, precision=highest)
    within_range = jnp.einsum(
        "ghts,sghp->tghp", scores[:, None] * damping, inputs_act, precision=highest
    )
    entering = (
        jnp.einsum("tgn,ghpn->tghp", reads_act, carried_state, precision=highest)
        * jnp.exp(cumulative)[..., None]
    )
    remaining = jnp.exp(cumulative[-1] - cumulative)
    new_state = jnp.exp(cumulative[-1])[..., None, None] * carried_state + jnp.einsum(
        "sgh,sghp,sgn->ghpn", remaining, inputs_act, writes_act, precision=highest
    )
    return (new_state, within_range + entering)


def split_rim(edges, first_width, second_width):
    return (
        edges[:, :first_width],
        edges[:, first_width : first_width + second_width],
        edges[:, first_width + second_width :],
    )


def shards(
    features, state_write, state_read, log_decay, conv_features, conv_write, conv_read, norm_gain
):
    tap_count = conv_features.shape[0]
    head_count = lax.axis_size("head")
    local_heads = H // head_count
    groups_here = G // head_count
    per_group = H // G
    moving = (features, state_write, state_read)
    inputs_act, writes_act, reads_act, decays = (
        lax.all_to_all(moving[0], "head", split_axis=1, concat_axis=0, tiled=True),
        lax.all_to_all(moving[1], "head", split_axis=1, concat_axis=0, tiled=True),
        lax.all_to_all(moving[2], "head", split_axis=1, concat_axis=0, tiled=True),
        lax.all_to_all(log_decay, "head", split_axis=1, concat_axis=0, tiled=True),
    )
    rim = jnp.concatenate(
        [
            inputs_act[-(tap_count - 1) :],
            writes_act[-(tap_count - 1) :],
            reads_act[-(tap_count - 1) :],
        ],
        1,
    )
    edges = passed_along(rim, "ctx", 1)
    lead_inputs, lead_writes, lead_reads = split_rim(
        edges, inputs_act.shape[1], writes_act.shape[1]
    )
    position = lax.axis_index("head")
    input_width = inputs_act.shape[1]
    state_width = writes_act.shape[1]
    inputs_act = causal_conv(
        inputs_act,
        lead_inputs,
        lax.dynamic_slice_in_dim(conv_features, position * input_width, input_width, 1),
    )
    writes_act = causal_conv(
        writes_act,
        lead_writes,
        lax.dynamic_slice_in_dim(conv_write, position * state_width, state_width, 1),
    )
    reads_act = causal_conv(
        reads_act,
        lead_reads,
        lax.dynamic_slice_in_dim(conv_read, position * state_width, state_width, 1),
    )
    length = inputs_act.shape[0]
    blocks = length // BLOCK
    blocked = (
        inputs_act.reshape(blocks, BLOCK, groups_here, per_group, P_SIZE),
        writes_act.reshape(blocks, BLOCK, groups_here, N),
        reads_act.reshape(blocks, BLOCK, groups_here, N),
        decays.reshape(blocks, BLOCK, groups_here, per_group),
    )
    initial = jnp.zeros((groups_here, per_group, P_SIZE, N), jnp.float32)
    final_state, partial_value = lax.scan(block_pass, initial, blocked)
    within = partial_value.reshape(length, groups_here, per_group, P_SIZE)
    decay_groups = decays.reshape(length, groups_here, per_group)
    segment_log = jnp.sum(decay_groups, 0)
    flattened = final_state.reshape(1, local_heads, P_SIZE * N)
    pieces = lax.all_to_all(flattened, "ctx", split_axis=2, concat_axis=0, tiled=True)
    totals = lax.all_gather(segment_log.reshape(1, local_heads), "ctx", axis=0, tiled=True)
    running = jnp.cumsum(totals, 0)
    segments = totals.shape[0]
    target = lax.broadcasted_iota(jnp.int32, (segments, segments), 0)
    source = lax.broadcasted_iota(jnp.int32, (segments, segments), 1)
    before = (source < target)[..., None]
    spacing = jnp.where(before, (running - totals)[:, None, :] - running[None, :, :], 0.0)
    weight = jnp.where(before, jnp.exp(spacing), 0.0)
    prefix = jnp.einsum("cdh,dhq->chq", weight, pieces, precision=highest)
    returned = lax.all_to_all(prefix, "ctx", split_axis=0, concat_axis=2, tiled=True)
    incoming = returned.reshape(groups_here, per_group, P_SIZE, N)
    rising = jnp.exp(jnp.cumsum(decay_groups, 0))
    carried = (
        jnp.einsum(
            "tgn,ghpn->tghp", reads_act.reshape(length, groups_here, N), incoming, precision=highest
        )
        * rising[..., None]
    )
    mixed = (within + carried).reshape(length, groups_here, per_group * P_SIZE)
    inverse = lax.rsqrt(jnp.mean(mixed * mixed, -1, keepdims=True) + eps_norm)
    return (mixed * inverse).reshape(length, local_heads * P_SIZE) * norm_gain


def solution(mesh):
    return jax.shard_map(
        shards,
        mesh=mesh,
        in_specs=(
            P(("ctx", "head"), None),
            P(("ctx", "head"), None),
            P(("ctx", "head"), None),
            P(("ctx", "head"), None),
            P(),
            P(),
            P(),
            P("head"),
        ),
        out_specs=P("ctx", "head"),
        check_vma=False,
    )
```

profile of v0, /device:TPU:26, one launch (start us, length us, event | category | flops | bytes accessed | tf_op | source)
XLA Modules:
  0.0 360.2 jit_solution(3611909566729080655)
XLA Ops:
  1.6 3.3 all-to-all-start.3
  9.0 3.5 all-to-all-start.1
  14.5 5.1 %all-to-all-done.1 = f32[128,2,512]{0,2,1:T(8,128)S(1)} async-done(((f32[128,2,512]{0,2,1:T(8,128)}), f32[128,2,512]{0,2,1:T(8,128)S(1)}, u32[]{:S(2)}, u32[]{:S(2)}) %all-to-all-start.1) | async-done | bytes 524320 | tf_op jit(solution)/shard_map/all_to_all | solution.py:77
  19.6 3.5 all-to-all-start.2
  23.0 5.6 %copy.51 = f32[128,8192]{0,1:T(8,128)} copy(f32[128,8192]{1,0:T(8,128)} %param.8) | data formatting | bytes 8388608 | tf_op args[0]
  29.6 5.8 %all-to-all-start = ((f32[128,2,4096]{0,2,1:T(8,128)}), f32[128,2,4096]{0,2,1:T(8,128)}, u32[]{:S(2)}, u32[]{:S(2)}) async-start(f32[128,2,4096]{0,2,1:T(8,128)} %bitcast.110), calls=%async_computation | async-start | bytes 8388608 | tf_op jit(solution)/shard_map/all_to_all | solution.py:76
  35.8 2.3 reduce-window.12
  39.1 40.9 %all-to-all-done = f32[128,2,4096]{0,2,1:T(8,128)} async-done(((f32[128,2,4096]{0,2,1:T(8,128)}), f32[128,2,4096]{0,2,1:T(8,128)}, u32[]{:S(2)}, u32[]{:S(2)}) %all-to-all-start) | async-done | bytes 4194336 | tf_op jit(solution)/shard_map/all_to_all | solution.py:76
  80.1 5.6 %copy.52 = f32[2,128,4096]{2,1,0:T(8,128)} copy(f32[2,128,4096]{1,2,0:T(8,128)} %bitcast.2) | data formatting | bytes 8388608 | tf_op jit(solution)/shard_map/all_to_all | solution.py:76
  86.6 2.1 collective-permute-start
  88.7 3.6 %collective-permute-done = f32[3,5120]{1,0:T(4,128)S(1)} collective-permute-done((f32[3,5120]{1,0:T(4,128)S(1)}, f32[3,5120]{1,0:T(4,128)S(1)}, u32[]{:S(2)}, u32[]{:S(2)}) %collective-permute-start) | collective-permute-done | bytes 61472 | tf_op jit(solution)/shard_map/ppermute | solution.py:20
  92.9 8.9 %divide_multiply_fusion = f32[256,4096]{1,0:T(8,128)} fusion(f32[256,4096]{1,0:T(8,128)} %bitcast.106, f32[3,4096]{1,0:T(4,128)S(1)} %slice.127, f32[4096]{0:T(1024)S(1)} %bitcast.131, f32[4096]{0:T(1024)S(1)} %bitcast.129, f32[4096]{0:T(1024)S(1)} %bitcast.130, f32[4096]{0:T(1024)S(1)} %bitcast.128), kind=kLoop, calls=%fused_computation.30 | loop fusion | flops 14680064 | bytes 8503296 | tf_op jit(solution)/shard_map/jit(silu)/mul | solution.py:30
  101.8 5.6 %copy.57 = f32[256,4096]{0,1:T(8,128)} copy(f32[256,4096]{1,0:T(8,128)} %divide_multiply_fusion) | data formatting | bytes 8388608 | tf_op jit(solution)/shard_map/jit(silu)/mul | solution.py:30
  107.4 7.3 %fusion.28 = f32[4,16,64,128]{3,2,1,0:T(8,128)} fusion(f32[256,4,128,1]{0,2,3,1:T(8,128)S(1)} %bitcast.118, f32[256,4,16,64]{0,3,2,1:T(8,128)} %bitcast.107, f32[256,4,16]{0,2,1:T(8,128)S(1)} %get-tuple-element.33, f32[4,16]{1,0:T(4,128)S(1)} %exponential_multiply_fusion), kind=kOutput, calls=%fused_computation.34 | convolution fusion | flops 1612185600 | bytes 6881536 | tf_op jit(solution)/shard_map/while/body/eval_jaxpr/sgh,sghp,sgn->ghpn/dot_general | solution.py:52
  116.5 6.6 %copy.68 = f32[1,64,8192]{1,0,2:T(1,128)} copy(f32[1,64,8192]{2,1,0:T(8,128)S(1)} %reshape.89) | data formatting | bytes 4194304 | tf_op jit(solution)/shard_map/reshape | solution.py:124
  123.5 38.3 %reduce.7 = f32[8192,64]{1,0:T(8,128)} reduce(f32[8192,1,64]{2,1,0:T(1,128)} %bitcast.112, f32[]{:T(128)} %broadcast.41), dimensions={1}, to_apply=%bitcast.91.reduce_sub_computation | reduce | bytes 4194308
  161.9 5.5 %reshape.104 = f32[16,1,32768]{2,1,0:T(1,128)} reshape(f32[8192,64]{1,0:T(8,128)} %reduce.7) | data formatting | bytes 4194304
  167.4 6.0 %all-to-all-start.4 = ((f32[16,1,32768]{2,1,0:T(1,128)}), f32[16,1,32768]{2,1,0:T(1,128)}, u32[]{:S(2)}, u32[]{:S(2)}) async-start(f32[16,1,32768]{2,1,0:T(1,128)} %reshape.104), calls=%async_computation.4 | async-start | bytes 4194304 | tf_op jit(solution)/shard_map/all_to_all | solution.py:125
  175.0 57.2 %all-reduce = f32[1024]{0:T(1024)S(1)} all-reduce(f32[1024]{0:T(1024)S(1)} %dynamic-update-slice), channel_id=2, replica_groups=mesh['ctx'=16,'head'=2] {'ctx'}, use_global_device_ids=true, to_apply=%add | all-reduce | flops 1024 | bytes 8192
  232.6 7.2 %reduce.8 = f32[16,32768]{1,0:T(8,128)S(1)} reduce(f32[16,1,32768]{2,1,0:T(1,128)} %all-to-all-done.4, f32[]{:T(128)} %broadcast.41), dimensions={1}, to_apply=%all_to_all.93.reduce_sub_computation | reduce | bytes 4194308 | tf_op jit(solution)/shard_map/all_to_all | solution.py:125
  239.8 6.6 %reshape.105 = f32[8192,1,64]{2,1,0:T(1,128)} reshape(f32[16,32768]{1,0:T(8,128)S(1)} %reduce.8) | data formatting | bytes 4194304
  246.3 3.4 copy.86
  251.8 2.5 copy.72
  254.3 11.1 %all-to-all-start.5 = ((f32[16,64,512]{2,1,0:T(8,128)}), f32[16,64,512]{2,1,0:T(8,128)S(1)}, u32[]{:S(2)}, u32[]{:S(2)}) async-start(f32[16,64,512]{2,1,0:T(8,128)} %copy.72), calls=%async_computation.5 | async-start | bytes 4194304 | tf_op jit(solution)/shard_map/all_to_all | solution.py:135
  269.9 4.9 %fusion.34 = f32[4,16,64,256]{3,2,1,0:T(8,128)} fusion(f32[256,4,128,1]{0,2,3,1:T(8,128)S(1)} %bitcast.116), kind=kOutput, calls=%fused_computation.36 | convolution fusion | flops 1610612736 | bytes 4718592 | tf_op jit(solution)/shard_map/while/body/eval_jaxpr/tgn,ghpn->tghp/dot_general | solution.py:48
  274.8 36.9 %all-to-all-done.5 = f32[16,64,512]{2,1,0:T(8,128)S(1)} async-done(((f32[16,64,512]{2,1,0:T(8,128)}), f32[16,64,512]{2,1,0:T(8,128)S(1)}, u32[]{:S(2)}, u32[]{:S(2)}) %all-to-all-start.5) | async-done | bytes 2097184 | tf_op jit(solution)/shard_map/all_to_all | solution.py:135
  311.6 2.5 copy.73
  315.8 3.4 fusion.67
  319.3 22.2 %multiply_reduce_fusion = (f32[256,4]{0,1:T(4,128)S(1)}, f32[256,4,16,64]{0,3,2,1:T(8,128)}) fusion(f32[4,16,64,256]{3,2,1,0:T(8,128)S(1)} %fusion.67, f32[256,4,16]{0,2,1:T(8,128)S(1)} %get-tuple-element.32, f32[4,16,64,256]{3,2,1,0:T(8,128)} %fusion.34, f32[256,4,16,64]{0,3,2,1:T(8,128)S(1)} %bitcast.108, f32[4,16,256]{2,1,0:T(8,128)S(1)} %get-tuple-element.34, ...), kind=kOutput, calls=%fused_computation.27 | convolution fusion | flops 3244293120 | bytes 18026496 | tf_op jit(solution)/shard_map/while/body/eval_jaxpr/ghts,sghp->tghp/dot_general | solution.py:44
  342.3 5.8 %copy.91 = f32[32,8,4,1024]{3,1,2,0:T(8,128)} copy(f32[32,8,4,1024]{3,2,1,0:T(4,128)S(1)} %bitcast.113) | data formatting | bytes 8388608
  348.1 5.6 %copy.76 = f32[256,4096]{1,0:T(8,128)} copy(f32[256,4096]{0,1:T(8,128)} %bitcast.120) | data formatting | bytes 8388608 | tf_op jit(solution)/shard_map/reshape | solution.py:144
  353.7 6.3 %multiply_multiply_fusion = f32[256,4096]{1,0:T(8,128)} fusion(f32[256,4096]{1,0:T(8,128)} %copy.76, f32[256,4096]{1,0:T(8,128)} %bitcast.111, f32[4096]{0:T(1024)S(1)} %copy-done.3), kind=kLoop, calls=%fused_computation.26 | loop fusion | flops 2097152 | bytes 12599296 | tf_op jit(solution)/shard_map/mul | solution.py:146
  (63 shorter events, 23.8 us)
Async XLA Ops:
  1.6 7.4 %all-to-all-start.3 = ((f32[128,2,64]{0,2,1:T(8,128)}), f32[128,2,64]{0,2,1:T(8,128)S(1)}, u32[]{:S(2)}, u32[]{:S(2)}) async-start(f32[128,2,64]{0,2,1:T(8,128)} %bitcast.24), calls=%async_computation.3 | async-start | bytes 131072 | tf_op jit(solution)/shard_map/all_to_all | solution.py:79
  9.0 10.6 %all-to-all-start.1 = ((f32[128,2,512]{0,2,1:T(8,128)}), f32[128,2,512]{0,2,1:T(8,128)S(1)}, u32[]{:S(2)}, u32[]{:S(2)}) async-start(f32[128,2,512]{0,2,1:T(8,128)} %bitcast.4), calls=%async_computation.1 | async-start | bytes 1048576 | tf_op jit(solution)/shard_map/all_to_all | solution.py:77
  19.6 10.1 %all-to-all-start.2 = ((f32[128,2,512]{0,2,1:T(8,128)}), f32[128,2,512]{0,2,1:T(8,128)S(1)}, u32[]{:S(2)}, u32[]{:S(2)}) async-start(f32[128,2,512]{0,2,1:T(8,128)} %bitcast.7), calls=%async_computation.2 | async-start | bytes 1048576 | tf_op jit(solution)/shard_map/all_to_all | solution.py:78
  29.6 5.8 %copy-start.4 = (f32[4,1024]{1,0:T(4,128)S(1)}, f32[4,1024]{1,0:T(4,128)}, u32[]{:S(2)}) copy-start(f32[4,1024]{1,0:T(4,128)} %param.14) | copy-start | bytes 49156
  29.6 5.8 %copy-start.5 = (f32[4,1024]{1,0:T(4,128)S(1)}, f32[4,1024]{1,0:T(4,128)}, u32[]{:S(2)}) copy-start(f32[4,1024]{1,0:T(4,128)} %param.13) | copy-start | bytes 49156
  29.6 5.9 %copy-start.2 = (f32[4,8192]{1,0:T(4,128)S(1)}, f32[4,8192]{1,0:T(4,128)}, u32[]{:S(2)}) copy-start(f32[4,8192]{1,0:T(4,128)} %param.12) | copy-start | bytes 393220
  29.6 50.5 %all-to-all-start = ((f32[128,2,4096]{0,2,1:T(8,128)}), f32[128,2,4096]{0,2,1:T(8,128)}, u32[]{:S(2)}, u32[]{:S(2)}) async-start(f32[128,2,4096]{0,2,1:T(8,128)} %bitcast.110), calls=%async_computation | async-start | bytes 8388608 | tf_op jit(solution)/shard_map/all_to_all | solution.py:76
  86.6 5.8 %collective-permute-start = (f32[3,5120]{1,0:T(4,128)S(1)}, f32[3,5120]{1,0:T(4,128)S(1)}, u32[]{:S(2)}, u32[]{:S(2)}) collective-permute-start(f32[3,5120]{1,0:T(4,128)S(1)} %pad_maximum_fusion.3), channel_id=1, source_target_pairs={{0,2},{2,4},{4,6},{6,8},{8,10},{10,12},{12,14},{14,16},{16,18},{18... | collective-permute-start | bytes 184328 | tf_op jit(solution)/shard_map/ppermute | solution.py:20
  161.9 11.5 %copy-start.6 = (u32[32]{0:T(128)S(1)}, u32[32]{0:T(128)}, u32[]{:S(2)}) copy-start(u32[32]{0:T(128)} %constant.53) | copy-start | bytes 388
  167.4 65.1 %all-to-all-start.4 = ((f32[16,1,32768]{2,1,0:T(1,128)}), f32[16,1,32768]{2,1,0:T(1,128)}, u32[]{:S(2)}, u32[]{:S(2)}) async-start(f32[16,1,32768]{2,1,0:T(1,128)} %reshape.104), calls=%async_computation.4 | async-start | bytes 4194304 | tf_op jit(solution)/shard_map/all_to_all | solution.py:125
  254.3 57.3 %all-to-all-start.5 = ((f32[16,64,512]{2,1,0:T(8,128)}), f32[16,64,512]{2,1,0:T(8,128)S(1)}, u32[]{:S(2)}, u32[]{:S(2)}) async-start(f32[16,64,512]{2,1,0:T(8,128)} %copy.72), calls=%async_computation.5 | async-start | bytes 4194304 | tf_op jit(solution)/shard_map/all_to_all | solution.py:135
  315.8 3.5 copy-start
  315.8 3.5 copy-start.1
  348.1 5.6 %copy-start.3 = (f32[4096]{0:T(1024)S(1)}, f32[4096]{0:T(1024)}, u32[]{:S(2)}) copy-start(f32[4096]{0:T(1024)} %param.15) | copy-start | bytes 49156
where the time goes:
time: 366 us; the launch traced here: 360 us
  waiting for transfers between devices  89.6 us (24%)
  local copies, waits for them, and re-layouts  70.1 us (19%)
  other arithmetic  64.9 us (18%)
  blocking collectives  57.2 us (16%)
  matrix products  42 us (11%)
  starting transfers between devices  35.3 us (10%)
    unnamed x1, blocking collectives  57.2 us
    all_to_all x1, waiting for transfers between devices, shards(): lax.all_to_all(moving[0], 'head', split_axis=1, concat_axis=0, tiled=True)  40.9 us
    unnamed x1, other arithmetic  38.3 us
    all_to_all x1, waiting for transfers between devices, shards(): lax.all_to_all(prefix, 'ctx', split_axis=0, concat_axis=2, tiled=True)  36.9 us
    unnamed x25, local copies, waits for them, and re-layouts  30.4 us
    dot_general x1, matrix products, block_pass(): jnp.einsum('ghts,sghp->tghp', scores[:, None] * damping, inputs_act, prec...  22.2 us
    all_to_all x1, starting transfers between devices, shards(): lax.all_to_all(prefix, 'ctx', split_axis=0, concat_axis=2, tiled=True)  11.1 us
    mul x3, other arithmetic, causal_conv(): return jax.nn.silu(summed)  10.3 us
  transfers between devices with their start and end apart: 7, of which 6 were waited for; matrix products, arithmetic and copies ran while one was open for 7% of the time, Pallas kernels for 0%

commit v1 on v0

v1 whole, which is shorter than its diff:
```python
import functools

import jax
import jax.numpy as jnp
from jax import lax
from jax.experimental import pallas as pl
from jax.experimental.pallas import tpu as pltpu
from jax.sharding import PartitionSpec as P

H = 128
P_SIZE = 64
N = 128
G = 8
CHUNK = 64
LANES = 256
EDGE = 8
PIECES = 3
MESH = pl.DeviceIdType.MESH
eps_norm = 1e-05
f32 = jnp.float32
bf16 = jnp.bfloat16


def split2(value):
    high = value.astype(bf16)
    return high, (value - high.astype(f32)).astype(bf16)


def split3(value):
    high = value.astype(bf16)
    rest = value - high.astype(f32)
    middle = rest.astype(bf16)
    return high, middle, (rest - middle.astype(f32)).astype(bf16)


def dot(a, b, dims=((1,), (0,))):
    return lax.dot_general(a, b, (dims, ((), ())), preferred_element_type=f32)


def dot3(a, b, dims=((1,), (0,))):
    return dot(a[0], b[0], dims) + (dot(a[0], b[1], dims) + dot(a[1], b[0], dims))


def silu(v):
    return v / (1.0 + jnp.exp(-v))


def conv(block, taps, extent):
    count = taps.shape[0]
    first = EDGE - (count - 1)
    summed = taps[0:1] * block[first : first + extent]
    for k in range(1, count):
        summed = summed + taps[k : k + 1] * block[first + k : first + k + extent]
    return silu(summed)


def kernel(
    nh,
    nc,
    x_hbm,
    w_hbm,
    r_hbm,
    l_hbm,
    cf_ref,
    cw_ref,
    cr_ref,
    out_hbm,
    xbuf,
    wbuf,
    rbuf,
    lbuf,
    yloc,
    cums,
    creads,
    gm,
    bt,
    sbuf,
    arecv,
    bsend,
    brecv,
    csend,
    crecv,
    dsend,
    inbuf,
    ysem,
    yrec,
    lsem,
    lrec,
    hsem,
    hrec,
    asem,
    arec,
    bsem,
    brec,
    csem,
    crec,
    dsem,
    drec,
    osem,
):
    c = lax.axis_index("ctx")
    h = lax.axis_index("head")
    groups = xbuf.shape[0]
    tl = x_hbm.shape[0]
    tokens = tl * nh
    width = xbuf.shape[2]
    heads_here = H // nh
    per_group = H // G
    core = c % 2
    side = (c // 2) % 2
    plane = c // 4
    planes = nc // 4
    core_peer = c + 1 - 2 * core
    side_peer = c + 2 - 4 * side

    barrier = pltpu.get_barrier_semaphore()

    def greet(ctx, head):
        pl.semaphore_signal(barrier, inc=1, device_id=(ctx, head), device_id_type=MESH)

    for d in range(1, nh):
        greet(c, (h + d) % nh)
    greet(core_peer, h)
    greet(side_peer, h)

    @pl.when(plane > 0)
    def _():
        greet(c - 4, h)

    @pl.when(plane < planes - 1)
    def _():
        greet(c + 4, h)

    @pl.when(c > 0)
    def _():
        greet(c - 1, nh - 1)

    gives_edge = jnp.logical_and(h == nh - 1, c < nc - 1)

    @pl.when(gives_edge)
    def _():
        for d in range(nh):
            greet(c + 1, d)

    below = (plane + planes - 1) // planes
    above = 1 - (plane + 1) // planes
    behind = (c + nc - 1) // nc
    ahead = ((h + 1) // nh) * (1 - (c + 1) // nc)
    pl.semaphore_wait(barrier, nh + 1 + below + above + behind + nh * ahead)

    kinds = ((x_hbm, xbuf, width), (w_hbm, wbuf, N), (r_hbm, rbuf, N))
    order = (1, 2, 0)

    def source(k, g, owner, start, rows):
        ref, _, wide = kinds[k]
        at = pl.multiple_of((owner * groups + g) * wide, wide)
        return ref.at[pl.ds(start, rows), pl.ds(at, wide)]

    def rows_of(owner):
        return pl.ds(pl.multiple_of(EDGE + owner * tl, 8), tl)

    def own_copy(k, g):
        return pltpu.make_async_copy(
            source(k, g, h, 0, tl), kinds[k][1].at[g, rows_of(h)], yrec.at[g, 0, k]
        )

    def head_copy(k, g, d, sender):
        return pltpu.make_async_remote_copy(
            src_ref=source(k, g, (h + d) % nh, 0, tl),
            dst_ref=kinds[k][1].at[g, rows_of(sender)],
            send_sem=ysem.at[g, d, k],
            recv_sem=yrec.at[g, d, k],
            device_id=(c, (h + d) % nh),
            device_id_type=MESH,
        )

    def decay_rows(owner):
        return lbuf.at[pl.ds(pl.multiple_of(owner * tl, 8), tl)]

    def decay_own():
        return pltpu.make_async_copy(l_hbm, decay_rows(h), lrec.at[0])

    def decay_copy(d, sender):
        return pltpu.make_async_remote_copy(
            src_ref=l_hbm,
            dst_ref=decay_rows(sender),
            send_sem=lsem.at[d],
            recv_sem=lrec.at[d],
            device_id=(c, (h + d) % nh),
            device_id_type=MESH,
        )

    def edge_copy(k, g, to):
        return pltpu.make_async_remote_copy(
            src_ref=source(k, g, to, tl - EDGE, EDGE),
            dst_ref=kinds[k][1].at[g, pl.ds(0, EDGE)],
            send_sem=hsem.at[g, to, k],
            recv_sem=hrec.at[g, k],
            device_id=(lax.rem(c + 1, nc), to),
            device_id_type=MESH,
        )

    decay_own().start()
    for d in range(1, nh):
        decay_copy(d, h).start()
    for g in range(groups):
        for k in order:
            own_copy(k, g).start()

        @pl.when(gives_edge)
        def _():
            for to in range(nh):
                for k in order:
                    edge_copy(k, g, to).start()

        for d in range(1, nh):
            for k in order:
                head_copy(k, g, d, h).start()

    @pl.when(c == 0)
    def _():
        for g in range(groups):
            for k in order:
                wide = kinds[k][2]
                kinds[k][1][g, 0:EDGE, :] = jnp.zeros((EDGE, wide), f32)

    decay_own().wait()
    for d in range(1, nh):
        decay_copy(d, (h - d + nh) % nh).wait_recv()
    target = lax.broadcasted_iota(jnp.int32, (tokens, tokens), 0)
    origin = lax.broadcasted_iota(jnp.int32, (tokens, tokens), 1)
    past = target >= origin
    near = jnp.logical_and(past, target // CHUNK == origin // CHUNK)
    decay3 = split3(lbuf[...])
    for which, mask in ((0, near), (1, past)):
        ones = jnp.where(mask, 1.0, 0.0).astype(bf16)
        total = dot(ones, decay3[0]) + dot(ones, decay3[1]) + dot(ones, decay3[2])
        for part, piece in enumerate(split3(total)):
            cums[which, part] = piece

    def spread(which, g, lane):
        head_at = lax.broadcasted_iota(jnp.int32, (H, LANES), 0)
        channel = lax.broadcasted_iota(jnp.int32, (H, LANES), 1)
        wanted = h * heads_here + g * per_group + (lane + channel) // P_SIZE
        ones = jnp.where(head_at == wanted, 1.0, 0.0).astype(bf16)
        return (
            dot(cums[which, 0], ones) + dot(cums[which, 1], ones) + dot(cums[which, 2], ones)
        )

    def peer_copy(src, dst, send, recv, ctx):
        return pltpu.make_async_remote_copy(
            src_ref=src,
            dst_ref=dst,
            send_sem=send,
            recv_sem=recv,
            device_id=(ctx, h),
            device_id_type=MESH,
        )

    piece_rows = sbuf.shape[2] // PIECES

    def rows_at(i):
        return pl.ds(i * piece_rows, piece_rows)

    def core_copy(g):
        return peer_copy(sbuf.at[g, 1 - core], arecv.at[g], asem.at[g], arec.at[g], core_peer)

    def side_copy(g, i):
        return peer_copy(
            bsend.at[g, rows_at(i)], brecv.at[g, rows_at(i)], bsem.at[g, i], brec.at[g, i], side_peer
        )

    def plane_copy(g, i):
        return peer_copy(
            csend.at[g, rows_at(i)],
            crecv.at[g, rows_at(i)],
            csem.at[g, i],
            crec.at[g, i],
            lax.rem(c + 4, nc),
        )

    def back_copy(g, i):
        return peer_copy(
            dsend.at[g, rows_at(i)],
            inbuf.at[g, core, rows_at(i)],
            dsem.at[g, i],
            drec.at[g, i],
            core_peer,
        )

    def back_arrival(g, i):
        return peer_copy(
            dsend.at[g, rows_at(i)],
            inbuf.at[g, 1 - core, rows_at(i)],
            dsem.at[g, i],
            drec.at[g, i],
            core_peer,
        )

    def local(g):
        for k in order:
            own_copy(k, g).wait()

        @pl.when(c > 0)
        def _():
            for k in order:
                edge_copy(k, g, 0).wait_recv()

        for d in range(1, nh):
            for k in order:
                head_copy(k, g, d, (h - d + nh) % nh).wait_recv()

        at = pl.multiple_of((h * groups + g) * N, N)
        writes = conv(wbuf[g], cw_ref[:, pl.ds(at, N)], tokens)
        reads = conv(rbuf[g], cr_ref[:, pl.ds(at, N)], tokens)
        reads2 = split2(reads)
        writes2 = split2(writes)
        creads[g, 0] = reads2[0]
        creads[g, 1] = reads2[1]
        row = lax.broadcasted_iota(jnp.int32, (CHUNK, CHUNK), 0)
        column = lax.broadcasted_iota(jnp.int32, (CHUNK, CHUNK), 1)
        for k in range(tokens // CHUNK):
            part = slice(k * CHUNK, (k + 1) * CHUNK)
            scores = dot3(
                (reads2[0][part], reads2[1][part]),
                (writes2[0][part], writes2[1][part]),
                ((1,), (1,)),
            )
            scores = split2(jnp.where(row >= column, scores, 0.0))
            gm[k, 0] = scores[0]
            gm[k, 1] = scores[1]
            turned = split2(jnp.transpose(writes[part]))
            bt[k, 0] = turned[0]
            bt[k, 1] = turned[1]

        def lanes(b, carry):
            lane = pl.multiple_of(b * LANES, LANES)
            cols = pl.ds(lane, LANES)
            taps = cf_ref[:, pl.ds(pl.multiple_of((h * groups + g) * width + lane, LANES), LANES)]
            spaced = spread(0, g, lane)
            state = None
            for k in range(tokens // CHUNK):
                part = slice(k * CHUNK, (k + 1) * CHUNK)
                act = conv(xbuf[g, k * CHUNK : k * CHUNK + CHUNK + EDGE, cols], taps, CHUNK)
                log = spaced[part]
                scaled = split2(act * jnp.exp(-log))
                mixed = dot3((gm[k, 0], gm[k, 1]), scaled)
                added = dot3((bt[k, 0], bt[k, 1]), scaled)
                if k > 0:
                    mixed = mixed + dot3((creads[g, 0, part], creads[g, 1, part]), split2(state))
                    added = added + state
                yloc[g, part, cols] = mixed * jnp.exp(log)
                state = added * jnp.exp(log[CHUNK - 1 : CHUNK])
            ends = spread(1, g, lane)[tokens - 1 : tokens]
            fade = jnp.broadcast_to(jnp.exp(ends), (EDGE, LANES))
            for half in range(2):
                sbuf[g, half, 0:EDGE, cols] = fade
                sbuf[g, half, EDGE : EDGE + N // 2, cols] = state[half * N // 2 : (half + 1) * N // 2]
            return carry

        lax.fori_loop(0, width // LANES, lanes, 0)
        core_copy(g).start()

    def pair(g):
        core_copy(g).wait_recv()
        mine_first = core == 0
        mine_fade = sbuf[g, core, 0:1]
        peer_fade = arecv[g, 0:1]
        late_fade = jnp.where(mine_first, peer_fade, mine_fade)
        for i in range(PIECES):
            rows = slice(i * piece_rows, (i + 1) * piece_rows)
            mine = sbuf[g, core, rows]
            peer = arecv[g, rows]
            first = jnp.where(mine_first, mine, peer)
            late = jnp.where(mine_first, peer, mine)
            bsend[g, rows] = late_fade * first + late
            if i == 0:
                bsend[g, 0:EDGE] = jnp.broadcast_to(mine_fade * peer_fade, (EDGE, width))
            side_copy(g, i).start()

    def chain(g):
        side_first = side == 0
        for i in range(PIECES):
            rows = slice(i * piece_rows, (i + 1) * piece_rows)
            side_copy(g, i).wait_recv()
            mine_fade = bsend[g, 0:1]
            peer_fade = brecv[g, 0:1]
            mine = bsend[g, rows]
            peer = brecv[g, rows]
            first = jnp.where(side_first, mine, peer)

            @pl.when(plane > 0)
            def _():
                plane_copy(g, i).wait_recv()

            @pl.when(plane == 0)
            def _():
                crecv[g, rows] = jnp.zeros((piece_rows, width), f32)

            entering = crecv[g, rows]

            @pl.when(plane < planes - 1)
            def _():
                late = jnp.where(side_first, peer, mine)
                late_fade = jnp.where(side_first, peer_fade, mine_fade)
                csend[g, rows] = (mine_fade * peer_fade) * entering + (late_fade * first + late)
                plane_copy(g, i).start()

            first_fade = jnp.where(side_first, mine_fade, peer_fade)
            even = jnp.where(side_first, entering, first_fade * entering + first)
            own = sbuf[g, core, rows]
            lead = jnp.where(core == 0, own, arecv[g, rows])
            lead_fade = jnp.where(core == 0, sbuf[g, core, 0:1], arecv[g, 0:1])
            odd = lead_fade * even + lead
            inbuf[g, core, rows] = jnp.where(core == 0, even, odd)
            dsend[g, rows] = jnp.where(core == 0, odd, even)
            back_copy(g, i).start()

    def out_copy(g):
        return pltpu.make_async_copy(
            yloc.at[g], out_hbm.at[:, pl.ds(pl.multiple_of(g * width, width), width)], osem.at[g]
        )

    def finish(g):
        for i in range(PIECES):
            back_arrival(g, i).wait_recv()

        def lanes(b, squares):
            lane = pl.multiple_of(b * LANES, LANES)
            cols = pl.ds(lane, LANES)
            state = jnp.concatenate(
                [
                    inbuf[g, 0, EDGE : EDGE + N // 2, cols],
                    inbuf[g, 1, EDGE : EDGE + N // 2, cols],
                ],
                0,
            )
            carried = dot3((creads[g, 0], creads[g, 1]), split2(state))
            mixed = yloc[g, :, cols] + carried * jnp.exp(spread(1, g, lane))
            yloc[g, :, cols] = mixed
            squared = mixed * mixed
            for at in range(0, LANES, 128):
                squares = squares + squared[:, at : at + 128]
            return squares

        squares = lax.fori_loop(0, width // LANES, lanes, jnp.zeros((tokens, 128), f32))
        inverse = lax.rsqrt(jnp.sum(squares, 1, keepdims=True) / width + eps_norm)
        yloc[g] = yloc[g] * inverse
        out_copy(g).start()

    def step(i, carry):
        @pl.when(i < groups)
        def _():
            local(i)
            pair(i)

        @pl.when(jnp.logical_and(i >= 1, i < groups + 1))
        def _():
            chain(i - 1)

        @pl.when(i >= 2)
        def _():
            finish(i - 2)

        return carry

    lax.fori_loop(0, groups + 2, step, 0)

    for d in range(1, nh):
        decay_copy(d, h).wait_send()
    for g in range(groups):
        out_copy(g).wait()
        core_copy(g).wait_send()
        for d in range(1, nh):
            for k in order:
                head_copy(k, g, d, h).wait_send()

        @pl.when(gives_edge)
        def _():
            for to in range(nh):
                for k in order:
                    edge_copy(k, g, to).wait_send()

        for i in range(PIECES):
            side_copy(g, i).wait_send()
            back_copy(g, i).wait_send()

            @pl.when(plane < planes - 1)
            def _():
                plane_copy(g, i).wait_send()


def shards(
    features, state_write, state_read, log_decay, conv_features, conv_write, conv_read, norm_gain
):
    nh = lax.axis_size("head")
    nc = lax.axis_size("ctx")
    groups = G // nh
    tokens = features.shape[0] * nh
    width = features.shape[1] // G
    half = N // 2 + EDGE
    count = tokens // CHUNK
    vm = pltpu.VMEM
    dma = pltpu.SemaphoreType.DMA
    anywhere = pl.BlockSpec(memory_space=pl.ANY)
    near = pl.BlockSpec(memory_space=pltpu.VMEM)
    mixed = pl.pallas_call(
        functools.partial(kernel, nh, nc),
        out_shape=jax.ShapeDtypeStruct((tokens, groups * width), f32),
        in_specs=[anywhere] * 4 + [near] * 3,
        out_specs=anywhere,
        scratch_shapes=[
            vm((groups, EDGE + tokens, width), f32),
            vm((groups, EDGE + tokens, N), f32),
            vm((groups, EDGE + tokens, N), f32),
            vm((tokens, H), f32),
            vm((groups, tokens, width), f32),
            vm((2, 3, tokens, H), bf16),
            vm((groups, 2, tokens, N), bf16),
            vm((count, 2, CHUNK, CHUNK), bf16),
            vm((count, 2, N, CHUNK), bf16),
            vm((groups, 2, half, width), f32),
            vm((groups, half, width), f32),
            vm((groups, half, width), f32),
            vm((groups, half, width), f32),
            vm((groups, half, width), f32),
            vm((groups, half, width), f32),
            vm((groups, half, width), f32),
            vm((groups, 2, half, width), f32),
            dma((groups, nh, 3)),
            dma((groups, nh, 3)),
            dma((nh,)),
            dma((nh,)),
            dma((groups, nh, 3)),
            dma((groups, 3)),
            dma((groups,)),
            dma((groups,)),
            dma((groups, PIECES)),
            dma((groups, PIECES)),
            dma((groups, PIECES)),
            dma((groups, PIECES)),
            dma((groups, PIECES)),
            dma((groups, PIECES)),
            dma((groups,)),
        ],
        compiler_params=pltpu.CompilerParams(
            collective_id=0, has_side_effects=True, vmem_limit_bytes=60 * 1024 * 1024
        ),
    )(features, state_write, state_read, log_decay, conv_features, conv_write, conv_read)
    return mixed * norm_gain


def solution(mesh):
    return jax.shard_map(
        shards,
        mesh=mesh,
        in_specs=(
            P(("ctx", "head"), None),
            P(("ctx", "head"), None),
            P(("ctx", "head"), None),
            P(("ctx", "head"), None),
            P(),
            P(),
            P(),
            P("head"),
        ),
        out_specs=P("ctx", "head"),
        check_vma=False,
    )
```

time: 366 us -> 104 us (0.28); the launches traced: 360 us -> 104 us
  Pallas kernels: 0 us -> 99 us
  waiting for transfers between devices: 89.6 us -> 0 us
  local copies, waits for them, and re-layouts: 70.1 us -> 0.01 us
  other arithmetic: 64.9 us -> 4.8 us
  blocking collectives: 57.2 us -> 0 us
  matrix products: 42 us -> 0 us
  starting transfers between devices: 35.3 us -> 0 us
    pallas_call x0 -> x1, Pallas kernels: none -> 99 us  [shards(): pl.pallas_call(functools.partial(kernel, nh, nc), out_shape=jax.ShapeDtyp...]
    all_to_all x6 -> x0, waiting for transfers between devices: 85.9 us -> none  [the longest x1 40.9 us: shards(): lax.all_to_all(moving[0], 'head', split_axis=1, concat_axis=0, tiled=True)]
    unnamed x1 -> x0, blocking collectives: 57.2 us -> none
    dot_general x6 -> x0, matrix products: 42 us -> none  [the longest x1 22.2 us: block_pass(): jnp.einsum('ghts,sghp->tghp', scores[:, None] * damping, inputs_act, prec...]
    unnamed x1 -> x0, other arithmetic: 38.3 us -> none
    all_to_all x6 -> x0, starting transfers between devices: 33.2 us -> none  [the longest x1 11.1 us: shards(): lax.all_to_all(prefix, 'ctx', split_axis=0, concat_axis=2, tiled=True)]
    unnamed x25 -> x2, local copies, waits for them, and re-layouts: 30.4 us -> 0.01 us
    reshape x5 -> x0, local copies, waits for them, and re-layouts: 15.6 us -> none  [the longest x2 8.32 us: shards(): flattened = final_state.reshape(1, local_heads, P_SIZE * N)]
  transfers between devices with their start and end apart: 7 -> 0, of which waited for: 6 -> 0; matrix products, arithmetic and copies ran while one was open for 7% -> 0% of each run, Pallas kernels for 0% -> 0%
where the time goes in v1:
time: 104 us
  Pallas kernels  99 us (95%)
  other arithmetic  4.8 us (5%)
    pallas_call x1, Pallas kernels, shards(): pl.pallas_call(functools.partial(kernel, nh, nc), out_shape=jax.ShapeDtyp...  99 us
    mul x1, other arithmetic, shards(): return mixed * norm_gain  4.8 us

profile of v1, /device:TPU:26, one launch (start us, length us, event | category | flops | bytes accessed | tf_op | source)
XLA Modules:
  0.0 103.8 jit_solution(10136097725266424797)
XLA Ops:
  0.0 0.0 copy-start
  0.0 99.0 %shard_map.82 = f32[256,4096]{1,0:T(8,128)} custom-call(f32[128,8192]{1,0:T(8,128)} %x_hbm.1, f32[128,1024]{1,0:T(8,128)} %w_hbm.1, f32[128,1024]{1,0:T(8,128)} %r_hbm.1, f32[128,128]{1,0:T(8,128)} %l_hbm.1, f32[4,8192]{1,0:T(4,128)} %cf_ref.1, f32[4,1024]{1,0:T(4,128)} %cw_ref.1, f32[4,1024]{1,0:T(4,128)} %cr_ref.1), custom_call_target="tpu_custom_call" | custom-call | tf_op jit(solution)/shard_map/pallas_call | solution.py:507
  99.0 0.0 copy-done
  99.0 4.8 %broadcast_multiply_fusion = f32[256,4096]{1,0:T(8,128)} fusion(f32[256,4096]{1,0:T(8,128)} %shard_map.82, f32[4096]{0:T(1024)S(1)} %copy-done), kind=kLoop, calls=%fused_computation | loop fusion | flops 1048576 | bytes 8404992 | tf_op jit(solution)/shard_map/mul | solution.py:550
Async XLA Ops:
  0.0 99.0 %copy-start = (f32[4096]{0:T(1024)S(1)}, f32[4096]{0:T(1024)}, u32[]{:S(2)}) copy-start(f32[4096]{0:T(1024)} %param.15) | copy-start | bytes 49156

commit v2 on v1

--- a/solution.py
+++ b/solution.py
@@ -15,6 +15,7 @@
 LANES = 256
 EDGE = 8
 PIECES = 3
+PARTS = 2
 MESH = pl.DeviceIdType.MESH
 eps_norm = 1e-05
 f32 = jnp.float32
@@ -71,6 +72,7 @@
     lbuf,
     yloc,
     cums,
+    squares_ref,
     creads,
     gm,
     bt,
@@ -100,12 +102,13 @@
 ):
     c = lax.axis_index("ctx")
     h = lax.axis_index("head")
-    groups = xbuf.shape[0]
+    units = xbuf.shape[0]
+    groups = units // PARTS
     tl = x_hbm.shape[0]
     tokens = tl * nh
     width = xbuf.shape[2]
     heads_here = H // nh
-    per_group = H // G
+    per_unit = H // G // PARTS
     core = c % 2
     side = (c // 2) % 2
     plane = c // 4
@@ -151,23 +154,33 @@
     kinds = ((x_hbm, xbuf, width), (w_hbm, wbuf, N), (r_hbm, rbuf, N))
     order = (1, 2, 0)
 
-    def source(k, g, owner, start, rows):
+    def kinds_of(u):
+        return order if u % PARTS == 0 else (0,)
+
+    def slot(k, u):
+        return u if k == 0 else u // PARTS
+
+    def source(k, u, owner, start, rows):
         ref, _, wide = kinds[k]
-        at = pl.multiple_of((owner * groups + g) * wide, wide)
+        place = owner * units + u if k == 0 else owner * groups + u // PARTS
+        at = pl.multiple_of(place * wide, wide)
         return ref.at[pl.ds(start, rows), pl.ds(at, wide)]
+
+    def landing(k, u, rows):
+        return kinds[k][1].at[slot(k, u), rows]
 
     def rows_of(owner):
         return pl.ds(pl.multiple_of(EDGE + owner * tl, 8), tl)
 
     def own_copy(k, g):
         return pltpu.make_async_copy(
-            source(k, g, h, 0, tl), kinds[k][1].at[g, rows_of(h)], yrec.at[g, 0, k]
+            source(k, g, h, 0, tl), landing(k, g, rows_of(h)), yrec.at[g, 0, k]
         )
 
     def head_copy(k, g, d, sender):
         return pltpu.make_async_remote_copy(
             src_ref=source(k, g, (h + d) % nh, 0, tl),
-            dst_ref=kinds[k][1].at[g, rows_of(sender)],
+            dst_ref=landing(k, g, rows_of(sender)),
             send_sem=ysem.at[g, d, k],
             recv_sem=yrec.at[g, d, k],
             device_id=(c, (h + d) % nh),
@@ -193,7 +206,7 @@
     def edge_copy(k, g, to):
         return pltpu.make_async_remote_copy(
             src_ref=source(k, g, to, tl - EDGE, EDGE),
-            dst_ref=kinds[k][1].at[g, pl.ds(0, EDGE)],
+            dst_ref=landing(k, g, pl.ds(0, EDGE)),
             send_sem=hsem.at[g, to, k],
             recv_sem=hrec.at[g, k],
             device_id=(lax.rem(c + 1, nc), to),
@@ -203,26 +216,26 @@
     decay_own().start()
     for d in range(1, nh):
         decay_copy(d, h).start()
-    for g in range(groups):
-        for k in order:
+    for g in range(units):
+        for k in kinds_of(g):
             own_copy(k, g).start()
 
         @pl.when(gives_edge)
         def _():
             for to in range(nh):
-                for k in order:
+                for k in kinds_of(g):
                     edge_copy(k, g, to).start()
 
         for d in range(1, nh):
-            for k in order:
+            for k in kinds_of(g):
                 head_copy(k, g, d, h).start()
 
     @pl.when(c == 0)
     def _():
-        for g in range(groups):
-            for k in order:
+        for g in range(units):
+            for k in kinds_of(g):
                 wide = kinds[k][2]
-                kinds[k][1][g, 0:EDGE, :] = jnp.zeros((EDGE, wide), f32)
+                kinds[k][1][slot(k, g), 0:EDGE, :] = jnp.zeros((EDGE, wide), f32)
 
     decay_own().wait()
     for d in range(1, nh):
@@ -241,7 +254,7 @@
     def spread(which, g, lane):
         head_at = lax.broadcasted_iota(jnp.int32, (H, LANES), 0)
         channel = lax.broadcasted_iota(jnp.int32, (H, LANES), 1)
-        wanted = h * heads_here + g * per_group + (lane + channel) // P_SIZE
+        wanted = h * heads_here + g * per_unit + (lane + channel) // P_SIZE
         ones = jnp.where(head_at == wanted, 1.0, 0.0).astype(bf16)
         return (
             dot(cums[which, 0], ones) + dot(cums[which, 1], ones) + dot(cums[which, 2], ones)
@@ -297,19 +310,20 @@
             core_peer,
         )
 
-    def local(g):
-        for k in order:
-            own_copy(k, g).wait()
+    def arrive(k, u):
+        own_copy(k, u).wait()
 
         @pl.when(c > 0)
         def _():
-            for k in order:
-                edge_copy(k, g, 0).wait_recv()
+            edge_copy(k, u, 0).wait_recv()
 
         for d in range(1, nh):
-            for k in order:
-                head_copy(k, g, d, (h - d + nh) % nh).wait_recv()
-
+            head_copy(k, u, d, (h - d + nh) % nh).wait_recv()
+
+    def project(u):
+        g = u // PARTS
+        for k in (1, 2):
+            arrive(k, u)
         at = pl.multiple_of((h * groups + g) * N, N)
         writes = conv(wbuf[g], cw_ref[:, pl.ds(at, N)], tokens)
         reads = conv(rbuf[g], cr_ref[:, pl.ds(at, N)], tokens)
@@ -333,15 +347,23 @@
             bt[k, 0] = turned[0]
             bt[k, 1] = turned[1]
 
+    def local(u):
+        @pl.when(u % PARTS == 0)
+        def _():
+            project(u)
+
+        g = u // PARTS
+        arrive(0, u)
+
         def lanes(b, carry):
             lane = pl.multiple_of(b * LANES, LANES)
             cols = pl.ds(lane, LANES)
-            taps = cf_ref[:, pl.ds(pl.multiple_of((h * groups + g) * width + lane, LANES), LANES)]
-            spaced = spread(0, g, lane)
+            taps = cf_ref[:, pl.ds(pl.multiple_of((h * units + u) * width + lane, LANES), LANES)]
+            spaced = spread(0, u, lane)
             state = None
             for k in range(tokens // CHUNK):
                 part = slice(k * CHUNK, (k + 1) * CHUNK)
-                act = conv(xbuf[g, k * CHUNK : k * CHUNK + CHUNK + EDGE, cols], taps, CHUNK)
+                act = conv(xbuf[u, k * CHUNK : k * CHUNK + CHUNK + EDGE, cols], taps, CHUNK)
                 log = spaced[part]
                 scaled = split2(act * jnp.exp(-log))
                 mixed = dot3((gm[k, 0], gm[k, 1]), scaled)
@@ -349,17 +371,17 @@
                 if k > 0:
                     mixed = mixed + dot3((creads[g, 0, part], creads[g, 1, part]), split2(state))
                     added = added + state
-                yloc[g, part, cols] = mixed * jnp.exp(log)
+                yloc[u, part, cols] = mixed * jnp.exp(log)
                 state = added * jnp.exp(log[CHUNK - 1 : CHUNK])
-            ends = spread(1, g, lane)[tokens - 1 : tokens]
+            ends = spread(1, u, lane)[tokens - 1 : tokens]
             fade = jnp.broadcast_to(jnp.exp(ends), (EDGE, LANES))
             for half in range(2):
-                sbuf[g, half, 0:EDGE, cols] = fade
-                sbuf[g, half, EDGE : EDGE + N // 2, cols] = state[half * N // 2 : (half + 1) * N // 2]
+                sbuf[u, half, 0:EDGE, cols] = fade
+                sbuf[u, half, EDGE : EDGE + N // 2, cols] = state[half * N // 2 : (half + 1) * N // 2]
             return carry
 
         lax.fori_loop(0, width // LANES, lanes, 0)
-        core_copy(g).start()
+        core_copy(u).start()
 
     def pair(g):
         core_copy(g).wait_recv()
@@ -421,64 +443,72 @@
             yloc.at[g], out_hbm.at[:, pl.ds(pl.multiple_of(g * width, width), width)], osem.at[g]
         )
 
-    def finish(g):
+    def finish(u):
+        g = u // PARTS
         for i in range(PIECES):
-            back_arrival(g, i).wait_recv()
+            back_arrival(u, i).wait_recv()
 
         def lanes(b, squares):
             lane = pl.multiple_of(b * LANES, LANES)
             cols = pl.ds(lane, LANES)
             state = jnp.concatenate(
                 [
-                    inbuf[g, 0, EDGE : EDGE + N // 2, cols],
-                    inbuf[g, 1, EDGE : EDGE + N // 2, cols],
+                    inbuf[u, 0, EDGE : EDGE + N // 2, cols],
+                    inbuf[u, 1, EDGE : EDGE + N // 2, cols],
                 ],
                 0,
             )
             carried = dot3((creads[g, 0], creads[g, 1]), split2(state))
-            mixed = yloc[g, :, cols] + carried * jnp.exp(spread(1, g, lane))
-            yloc[g, :, cols] = mixed
+            mixed = yloc[u, :, cols] + carried * jnp.exp(spread(1, u, lane))
+            yloc[u, :, cols] = mixed
             squared = mixed * mixed
             for at in range(0, LANES, 128):
                 squares = squares + squared[:, at : at + 128]
             return squares
 
-        squares = lax.fori_loop(0, width // LANES, lanes, jnp.zeros((tokens, 128), f32))
-        inverse = lax.rsqrt(jnp.sum(squares, 1, keepdims=True) / width + eps_norm)
-        yloc[g] = yloc[g] * inverse
-        out_copy(g).start()
+        before = jnp.where(u % PARTS == 0, 0.0, 1.0) * squares_ref[...]
+        squares_ref[...] = lax.fori_loop(0, width // LANES, lanes, before)
+
+        @pl.when(u % PARTS == PARTS - 1)
+        def _():
+            mean = jnp.sum(squares_ref[...], 1, keepdims=True) / (width * PARTS)
+            inverse = lax.rsqrt(mean + eps_norm)
+            for back in range(PARTS - 1, -1, -1):
+                yloc[u - back] = yloc[u - back] * inverse
+                out_copy(u - back).start()
 
     def step(i, carry):
-        @pl.when(i < groups)
+        @pl.when(i < units)
         def _():
             local(i)
             pair(i)
 
-        @pl.when(jnp.logical_and(i >= 1, i < groups + 1))
+        @pl.when(i >= 2)
+        def _():
+            finish(i - 2)
+
+        @pl.when(jnp.logical_and(i >= 1, i < units + 1))
         def _():
             chain(i - 1)
 
-        @pl.when(i >= 2)
-        def _():
-            finish(i - 2)
-
         return carry
 
-    lax.fori_loop(0, groups + 2, step, 0)
+    squares_ref[...] = jnp.zeros((tokens, 128), f32)
+    lax.fori_loop(0, units + 2, step, 0)
 
     for d in range(1, nh):
         decay_copy(d, h).wait_send()
-    for g in range(groups):
+    for g in range(units):
         out_copy(g).wait()
         core_copy(g).wait_send()
         for d in range(1, nh):
-            for k in order:
+            for k in kinds_of(g):
                 head_copy(k, g, d, h).wait_send()
 
         @pl.when(gives_edge)
         def _():
             for to in range(nh):
-                for k in order:
+                for k in kinds_of(g):
                     edge_copy(k, g, to).wait_send()
 
         for i in range(PIECES):
@@ -496,8 +526,9 @@
     nh = lax.axis_size("head")
     nc = lax.axis_size("ctx")
     groups = G // nh
+    units = groups * PARTS
     tokens = features.shape[0] * nh
-    width = features.shape[1] // G
+    width = features.shape[1] // (G * PARTS)
     half = N // 2 + EDGE
     count = tokens // CHUNK
     vm = pltpu.VMEM
@@ -506,42 +537,43 @@
     near = pl.BlockSpec(memory_space=pltpu.VMEM)
     mixed = pl.pallas_call(
         functools.partial(kernel, nh, nc),
-        out_shape=jax.ShapeDtypeStruct((tokens, groups * width), f32),
+        out_shape=jax.ShapeDtypeStruct((tokens, units * width), f32),
         in_specs=[anywhere] * 4 + [near] * 3,
         out_specs=anywhere,
         scratch_shapes=[
-            vm((groups, EDGE + tokens, width), f32),
+            vm((units, EDGE + tokens, width), f32),
             vm((groups, EDGE + tokens, N), f32),
             vm((groups, EDGE + tokens, N), f32),
             vm((tokens, H), f32),
-            vm((groups, tokens, width), f32),
+            vm((units, tokens, width), f32),
             vm((2, 3, tokens, H), bf16),
+            vm((tokens, 128), f32),
             vm((groups, 2, tokens, N), bf16),
             vm((count, 2, CHUNK, CHUNK), bf16),
             vm((count, 2, N, CHUNK), bf16),
-            vm((groups, 2, half, width), f32),
-            vm((groups, half, width), f32),
-            vm((groups, half, width), f32),
-            vm((groups, half, width), f32),
-            vm((groups, half, width), f32),
-            vm((groups, half, width), f32),
-            vm((groups, half, width), f32),
-            vm((groups, 2, half, width), f32),
-            dma((groups, nh, 3)),
-            dma((groups, nh, 3)),
+            vm((units, 2, half, width), f32),
+            vm((units, half, width), f32),
+            vm((units, half, width), f32),
+            vm((units, half, width), f32),
+            vm((units, half, width), f32),
+            vm((units, half, width), f32),
+            vm((units, half, width), f32),
+            vm((units, 2, half, width), f32),
+            dma((units, nh, 3)),
+            dma((units, nh, 3)),
             dma((nh,)),
             dma((nh,)),
-            dma((groups, nh, 3)),
-            dma((groups, 3)),
-            dma((groups,)),
-            dma((groups,)),
-            dma((groups, PIECES)),
-            dma((groups, PIECES)),
-            dma((groups, PIECES)),
-            dma((groups, PIECES)),
-            dma((groups, PIECES)),
-            dma((groups, PIECES)),
-            dma((groups,)),
+            dma((units, nh, 3)),
+            dma((units, 3)),
+            dma((units,)),
+            dma((units,)),
+            dma((units, PIECES)),
+            dma((units, PIECES)),
+            dma((units, PIECES)),
+            dma((units, PIECES)),
+            dma((units, PIECES)),
+            dma((units, PIECES)),
+            dma((units,)),
         ],
         compiler_params=pltpu.CompilerParams(
             collective_id=0, has_side_effects=True, vmem_limit_bytes=60 * 1024 * 1024

time: 104 us -> 96.6 us (0.929)
  Pallas kernels: 99 us -> 91 us
    pallas_call x1, Pallas kernels: 99 us -> 91 us  [shards(): pl.pallas_call(functools.partial(kernel, nh, nc), out_shape=jax.ShapeDtyp...]
where the time goes in v2:
time: 96.6 us; the launch traced here: 95.8 us
  Pallas kernels  91 us (94%)
  other arithmetic  4.8 us (5%)
    pallas_call x1, Pallas kernels, shards(): pl.pallas_call(functools.partial(kernel, nh, nc), out_shape=jax.ShapeDtyp...  91 us
    mul x1, other arithmetic, shards(): return mixed * norm_gain  4.8 us

profile of v2, /device:TPU:26, one launch (start us, length us, event | category | flops | bytes accessed | tf_op | source)
XLA Modules:
  0.0 95.8 jit_solution(16623874430888662384)
XLA Ops:
  0.0 0.0 copy-start
  0.0 91.0 %shard_map.82 = f32[256,4096]{1,0:T(8,128)} custom-call(f32[128,8192]{1,0:T(8,128)} %x_hbm.1, f32[128,1024]{1,0:T(8,128)} %w_hbm.1, f32[128,1024]{1,0:T(8,128)} %r_hbm.1, f32[128,128]{1,0:T(8,128)} %l_hbm.1, f32[4,8192]{1,0:T(4,128)} %cf_ref.1, f32[4,1024]{1,0:T(4,128)} %cw_ref.1, f32[4,1024]{1,0:T(4,128)} %cr_ref.1), custom_call_target="tpu_custom_call" | custom-call | tf_op jit(solution)/shard_map/pallas_call | solution.py:538
  91.0 0.0 copy-done
  91.0 4.8 %broadcast_multiply_fusion = f32[256,4096]{1,0:T(8,128)} fusion(f32[256,4096]{1,0:T(8,128)} %shard_map.82, f32[4096]{0:T(1024)S(1)} %copy-done), kind=kLoop, calls=%fused_computation | loop fusion | flops 1048576 | bytes 8404992 | tf_op jit(solution)/shard_map/mul | solution.py:582
Async XLA Ops:
  0.0 91.0 %copy-start = (f32[4096]{0:T(1024)S(1)}, f32[4096]{0:T(1024)}, u32[]{:S(2)}) copy-start(f32[4096]{0:T(1024)} %param.15) | copy-start | bytes 49156

commit v3 on v2

--- a/solution.py
+++ b/solution.py
@@ -14,7 +14,7 @@
 CHUNK = 64
 LANES = 256
 EDGE = 8
-PIECES = 3
+PIECES = 9
 PARTS = 2
 MESH = pl.DeviceIdType.MESH
 eps_norm = 1e-05
@@ -65,7 +65,7 @@
     cf_ref,
     cw_ref,
     cr_ref,
-    out_hbm,
+    out_ref,
     xbuf,
     wbuf,
     rbuf,
@@ -98,7 +98,6 @@
     crec,
     dsem,
     drec,
-    osem,
 ):
     c = lax.axis_index("ctx")
     h = lax.axis_index("head")
@@ -136,20 +135,19 @@
 
     @pl.when(c > 0)
     def _():
-        greet(c - 1, nh - 1)
-
-    gives_edge = jnp.logical_and(h == nh - 1, c < nc - 1)
+        greet(c - 1, h)
+
+    gives_edge = c < nc - 1
 
     @pl.when(gives_edge)
     def _():
-        for d in range(nh):
-            greet(c + 1, d)
+        greet(c + 1, h)
 
     below = (plane + planes - 1) // planes
     above = 1 - (plane + 1) // planes
     behind = (c + nc - 1) // nc
-    ahead = ((h + 1) // nh) * (1 - (c + 1) // nc)
-    pl.semaphore_wait(barrier, nh + 1 + below + above + behind + nh * ahead)
+    ahead = 1 - (c + 1) // nc
+    pl.semaphore_wait(barrier, nh + 1 + below + above + behind + ahead)
 
     kinds = ((x_hbm, xbuf, width), (w_hbm, wbuf, N), (r_hbm, rbuf, N))
     order = (1, 2, 0)
@@ -169,20 +167,24 @@
     def landing(k, u, rows):
         return kinds[k][1].at[slot(k, u), rows]
 
-    def rows_of(owner):
-        return pl.ds(pl.multiple_of(EDGE + owner * tl, 8), tl)
-
-    def own_copy(k, g):
+    def rows_of(owner, edge):
+        start = EDGE + owner * tl + edge * (tl - EDGE)
+        return pl.ds(pl.multiple_of(start, 8), EDGE if edge else tl - EDGE)
+
+    def taken(k, u, owner, edge):
+        return source(k, u, owner, edge * (tl - EDGE), EDGE if edge else tl - EDGE)
+
+    def own_copy(k, u, edge):
         return pltpu.make_async_copy(
-            source(k, g, h, 0, tl), landing(k, g, rows_of(h)), yrec.at[g, 0, k]
-        )
-
-    def head_copy(k, g, d, sender):
+            taken(k, u, h, edge), landing(k, u, rows_of(h, edge)), yrec.at[u, 0, k + 3 * edge]
+        )
+
+    def head_copy(k, u, d, sender, edge):
         return pltpu.make_async_remote_copy(
-            src_ref=source(k, g, (h + d) % nh, 0, tl),
-            dst_ref=landing(k, g, rows_of(sender)),
-            send_sem=ysem.at[g, d, k],
-            recv_sem=yrec.at[g, d, k],
+            src_ref=taken(k, u, (h + d) % nh, edge),
+            dst_ref=landing(k, u, rows_of(sender, edge)),
+            send_sem=ysem.at[u, d, k + 3 * edge],
+            recv_sem=yrec.at[u, d, k + 3 * edge],
             device_id=(c, (h + d) % nh),
             device_id_type=MESH,
         )
@@ -203,32 +205,25 @@
             device_id_type=MESH,
         )
 
-    def edge_copy(k, g, to):
+    def edge_copy(k, u):
         return pltpu.make_async_remote_copy(
-            src_ref=source(k, g, to, tl - EDGE, EDGE),
-            dst_ref=landing(k, g, pl.ds(0, EDGE)),
-            send_sem=hsem.at[g, to, k],
-            recv_sem=hrec.at[g, k],
-            device_id=(lax.rem(c + 1, nc), to),
+            src_ref=landing(k, u, pl.ds(tokens, EDGE)),
+            dst_ref=landing(k, u, pl.ds(0, EDGE)),
+            send_sem=hsem.at[u, k],
+            recv_sem=hrec.at[u, k],
+            device_id=(lax.rem(c + 1, nc), h),
             device_id_type=MESH,
         )
 
     decay_own().start()
     for d in range(1, nh):
         decay_copy(d, h).start()
-    for g in range(units):
-        for k in kinds_of(g):
-            own_copy(k, g).start()
-
-        @pl.when(gives_edge)
-        def _():
-            for to in range(nh):
-                for k in kinds_of(g):
-                    edge_copy(k, g, to).start()
-
-        for d in range(1, nh):
-            for k in kinds_of(g):
-                head_copy(k, g, d, h).start()
+    for edge in (1, 0):
+        for u in range(units):
+            for k in kinds_of(u):
+                own_copy(k, u, edge).start()
+                for d in range(1, nh):
+                    head_copy(k, u, d, h, edge).start()
 
     @pl.when(c == 0)
     def _():
@@ -251,6 +246,22 @@
         for part, piece in enumerate(split3(total)):
             cums[which, part] = piece
 
+    last = (h + 1) % nh
+    for u in range(units):
+        for k in kinds_of(u):
+
+            @pl.when(h == nh - 1)
+            def _():
+                own_copy(k, u, 1).wait()
+
+            @pl.when(h < nh - 1)
+            def _():
+                head_copy(k, u, last, nh - 1, 1).wait_recv()
+
+            @pl.when(gives_edge)
+            def _():
+                edge_copy(k, u).start()
+
     def spread(which, g, lane):
         head_at = lax.broadcasted_iota(jnp.int32, (H, LANES), 0)
         channel = lax.broadcasted_iota(jnp.int32, (H, LANES), 1)
@@ -311,14 +322,22 @@
         )
 
     def arrive(k, u):
-        own_copy(k, u).wait()
+        own_copy(k, u, 0).wait()
 
         @pl.when(c > 0)
         def _():
-            edge_copy(k, u, 0).wait_recv()
+            edge_copy(k, u).wait_recv()
+
+        @pl.when(h < nh - 1)
+        def _():
+            own_copy(k, u, 1).wait()
 
         for d in range(1, nh):
-            head_copy(k, u, d, (h - d + nh) % nh).wait_recv()
+            head_copy(k, u, d, (h - d + nh) % nh, 0).wait_recv()
+
+            @pl.when(d != last)
+            def _():
+                head_copy(k, u, d, (h - d + nh) % nh, 1).wait_recv()
 
     def project(u):
         g = u // PARTS
@@ -438,11 +457,6 @@
             dsend[g, rows] = jnp.where(core == 0, odd, even)
             back_copy(g, i).start()
 
-    def out_copy(g):
-        return pltpu.make_async_copy(
-            yloc.at[g], out_hbm.at[:, pl.ds(pl.multiple_of(g * width, width), width)], osem.at[g]
-        )
-
     def finish(u):
         g = u // PARTS
         for i in range(PIECES):
@@ -474,8 +488,8 @@
             mean = jnp.sum(squares_ref[...], 1, keepdims=True) / (width * PARTS)
             inverse = lax.rsqrt(mean + eps_norm)
             for back in range(PARTS - 1, -1, -1):
-                yloc[u - back] = yloc[u - back] * inverse
-                out_copy(u - back).start()
+                cols = pl.ds(pl.multiple_of((u - back) * width, width), width)
+                out_ref[:, cols] = yloc[u - back] * inverse
 
     def step(i, carry):
         @pl.when(i < units)
@@ -499,17 +513,16 @@
     for d in range(1, nh):
         decay_copy(d, h).wait_send()
     for g in range(units):
-        out_copy(g).wait()
         core_copy(g).wait_send()
         for d in range(1, nh):
             for k in kinds_of(g):
-                head_copy(k, g, d, h).wait_send()
+                head_copy(k, g, d, h, 0).wait_send()
+                head_copy(k, g, d, h, 1).wait_send()
 
         @pl.when(gives_edge)
         def _():
-            for to in range(nh):
-                for k in kinds_of(g):
-                    edge_copy(k, g, to).wait_send()
+            for k in kinds_of(g):
+                edge_copy(k, g).wait_send()
 
         for i in range(PIECES):
             side_copy(g, i).wait_send()
@@ -537,9 +550,9 @@
     near = pl.BlockSpec(memory_space=pltpu.VMEM)
     mixed = pl.pallas_call(
         functools.partial(kernel, nh, nc),
-        out_shape=jax.ShapeDtypeStruct((tokens, units * width), f32),
+        out_shape=pltpu.VMEM((tokens, units * width), f32),
         in_specs=[anywhere] * 4 + [near] * 3,
-        out_specs=anywhere,
+        out_specs=near,
         scratch_shapes=[
             vm((units, EDGE + tokens, width), f32),
             vm((groups, EDGE + tokens, N), f32),
@@ -559,11 +572,11 @@
             vm((units, half, width), f32),
             vm((units, half, width), f32),
             vm((units, 2, half, width), f32),
-            dma((units, nh, 3)),
-            dma((units, nh, 3)),
+            dma((units, nh, 6)),
+            dma((units, nh, 6)),
             dma((nh,)),
             dma((nh,)),
-            dma((units, nh, 3)),
+            dma((units, 3)),
             dma((units, 3)),
             dma((units,)),
             dma((units,)),
@@ -573,10 +586,9 @@
             dma((units, PIECES)),
             dma((units, PIECES)),
             dma((units, PIECES)),
-            dma((units,)),
         ],
         compiler_params=pltpu.CompilerParams(
-            collective_id=0, has_side_effects=True, vmem_limit_bytes=60 * 1024 * 1024
+            collective_id=0, has_side_effects=True, vmem_limit_bytes=58 * 1024 * 1024
         ),
     )(features, state_write, state_read, log_decay, conv_features, conv_write, conv_read)
     return mixed * norm_gain

time: 96.6 us -> 92.9 us (0.962)
  other arithmetic: 4.8 us -> 2.61 us
  Pallas kernels: 91 us -> 89.6 us
    mul x1, other arithmetic: 4.8 us -> 2.61 us  [shards(): return mixed * norm_gain]
    pallas_call x1, Pallas kernels: 91 us -> 89.6 us  [shards(): pl.pallas_call(functools.partial(kernel, nh, nc), out_shape=pltpu.VMEM((t...]
where the time goes in v3:
time: 92.9 us; the launch traced here: 92.2 us
  Pallas kernels  89.6 us (96%)
  other arithmetic  2.61 us (3%)
    pallas_call x1, Pallas kernels, shards(): pl.pallas_call(functools.partial(kernel, nh, nc), out_shape=pltpu.VMEM((t...  89.6 us
    mul x1, other arithmetic, shards(): return mixed * norm_gain  2.61 us

profile of v3, /device:TPU:26, one launch (start us, length us, event | category | flops | bytes accessed | tf_op | source)
XLA Modules:
  0.0 92.2 jit_solution(173455821275709889)
XLA Ops:
  0.0 0.0 copy-start
  0.0 89.6 %shard_map.82 = f32[256,4096]{1,0:T(8,128)S(1)} custom-call(f32[128,8192]{1,0:T(8,128)} %x_hbm.1, f32[128,1024]{1,0:T(8,128)} %w_hbm.1, f32[128,1024]{1,0:T(8,128)} %r_hbm.1, f32[128,128]{1,0:T(8,128)} %l_hbm.1, f32[4,8192]{1,0:T(4,128)} %cf_ref.1, f32[4,1024]{1,0:T(4,128)} %cw_ref.1, f32[4,1024]{1,0:T(4,128)} %cr_ref.1), custom_call_target="tpu_custom_call" | custom-call | tf_op jit(solution)/shard_map/pallas_call | solution.py:551
  89.6 0.0 copy-done
  89.6 2.6 %broadcast_multiply_fusion = f32[256,4096]{1,0:T(8,128)} fusion(f32[256,4096]{1,0:T(8,128)S(1)} %shard_map.82, f32[4096]{0:T(1024)S(1)} %copy-done), kind=kLoop, calls=%fused_computation | loop fusion | flops 1048576 | bytes 8404992 | tf_op jit(solution)/shard_map/mul | solution.py:594
Async XLA Ops:
  0.0 89.6 %copy-start = (f32[4096]{0:T(1024)S(1)}, f32[4096]{0:T(1024)}, u32[]{:S(2)}) copy-start(f32[4096]{0:T(1024)} %param.15) | copy-start | bytes 49156

commit v4 on v3

--- a/solution.py
+++ b/solution.py
@@ -14,7 +14,7 @@
 CHUNK = 64
 LANES = 256
 EDGE = 8
-PIECES = 9
+PIECES = 3
 PARTS = 2
 MESH = pl.DeviceIdType.MESH
 eps_norm = 1e-05
@@ -424,34 +424,39 @@
         for i in range(PIECES):
             rows = slice(i * piece_rows, (i + 1) * piece_rows)
             side_copy(g, i).wait_recv()
-            mine_fade = bsend[g, 0:1]
-            peer_fade = brecv[g, 0:1]
-            mine = bsend[g, rows]
-            peer = brecv[g, rows]
-            first = jnp.where(side_first, mine, peer)
+
+            @pl.when(plane == 0)
+            def _():
+                crecv[g, rows] = jnp.zeros((piece_rows, width), f32)
 
             @pl.when(plane > 0)
             def _():
                 plane_copy(g, i).wait_recv()
 
-            @pl.when(plane == 0)
-            def _():
-                crecv[g, rows] = jnp.zeros((piece_rows, width), f32)
-
-            entering = crecv[g, rows]
-
             @pl.when(plane < planes - 1)
             def _():
+                mine_fade = bsend[g, 0:1]
+                peer_fade = brecv[g, 0:1]
+                mine = bsend[g, rows]
+                peer = brecv[g, rows]
+                first = jnp.where(side_first, mine, peer)
                 late = jnp.where(side_first, peer, mine)
                 late_fade = jnp.where(side_first, peer_fade, mine_fade)
-                csend[g, rows] = (mine_fade * peer_fade) * entering + (late_fade * first + late)
+                csend[g, rows] = (mine_fade * peer_fade) * crecv[g, rows] + (
+                    late_fade * first + late
+                )
                 plane_copy(g, i).start()
 
-            first_fade = jnp.where(side_first, mine_fade, peer_fade)
+        mine_fade = bsend[g, 0:1]
+        peer_fade = brecv[g, 0:1]
+        first_fade = jnp.where(side_first, mine_fade, peer_fade)
+        lead_fade = jnp.where(core == 0, sbuf[g, core, 0:1], arecv[g, 0:1])
+        for i in range(PIECES):
+            rows = slice(i * piece_rows, (i + 1) * piece_rows)
+            first = jnp.where(side_first, bsend[g, rows], brecv[g, rows])
+            entering = crecv[g, rows]
             even = jnp.where(side_first, entering, first_fade * entering + first)
-            own = sbuf[g, core, rows]
-            lead = jnp.where(core == 0, own, arecv[g, rows])
-            lead_fade = jnp.where(core == 0, sbuf[g, core, 0:1], arecv[g, 0:1])
+            lead = jnp.where(core == 0, sbuf[g, core, rows], arecv[g, rows])
             odd = lead_fade * even + lead
             inbuf[g, core, rows] = jnp.where(core == 0, even, odd)
             dsend[g, rows] = jnp.where(core == 0, odd, even)
@@ -497,13 +502,13 @@
             local(i)
             pair(i)
 
+        @pl.when(jnp.logical_and(i >= 1, i < units + 1))
+        def _():
+            chain(i - 1)
+
         @pl.when(i >= 2)
         def _():
             finish(i - 2)
-
-        @pl.when(jnp.logical_and(i >= 1, i < units + 1))
-        def _():
-            chain(i - 1)
 
         return carry
 

time: 92.9 us -> 90.2 us (0.971); the launches traced: 92.2 us -> 88.6 us
  Pallas kernels: 89.6 us -> 85.9 us
    pallas_call x1, Pallas kernels: 89.6 us -> 85.9 us  [shards(): pl.pallas_call(functools.partial(kernel, nh, nc), out_shape=pltpu.VMEM((t...]
where the time goes in v4:
time: 90.2 us; the launch traced here: 88.6 us
  Pallas kernels  85.9 us (95%)
  other arithmetic  2.61 us (3%)
    pallas_call x1, Pallas kernels, shards(): pl.pallas_call(functools.partial(kernel, nh, nc), out_shape=pltpu.VMEM((t...  85.9 us
    mul x1, other arithmetic, shards(): return mixed * norm_gain  2.61 us

profile of v4, /device:TPU:26, one launch (start us, length us, event | category | flops | bytes accessed | tf_op | source)
XLA Modules:
  0.0 88.6 jit_solution(4568638155798893122)
XLA Ops:
  0.0 0.0 copy-start
  0.0 85.9 %shard_map.82 = f32[256,4096]{1,0:T(8,128)S(1)} custom-call(f32[128,8192]{1,0:T(8,128)} %x_hbm.1, f32[128,1024]{1,0:T(8,128)} %w_hbm.1, f32[128,1024]{1,0:T(8,128)} %r_hbm.1, f32[128,128]{1,0:T(8,128)} %l_hbm.1, f32[4,8192]{1,0:T(4,128)} %cf_ref.1, f32[4,1024]{1,0:T(4,128)} %cw_ref.1, f32[4,1024]{1,0:T(4,128)} %cr_ref.1), custom_call_target="tpu_custom_call" | custom-call | tf_op jit(solution)/shard_map/pallas_call | solution.py:556
  85.9 0.0 copy-done
  86.0 2.6 %broadcast_multiply_fusion = f32[256,4096]{1,0:T(8,128)} fusion(f32[256,4096]{1,0:T(8,128)S(1)} %shard_map.82, f32[4096]{0:T(1024)S(1)} %copy-done), kind=kLoop, calls=%fused_computation | loop fusion | flops 1048576 | bytes 8404992 | tf_op jit(solution)/shard_map/mul | solution.py:599
Async XLA Ops:
  0.0 86.0 %copy-start = (f32[4096]{0:T(1024)S(1)}, f32[4096]{0:T(1024)}, u32[]{:S(2)}) copy-start(f32[4096]{0:T(1024)} %param.15) | copy-start | bytes 49156
